TPU v7x, 32 devices: a whole 2x2x4 slice. The times are simulated.
32 devices in a mesh: tm: 2 (over y), height: 16 (over z, x, core).
Axes of the slice: x: 2, y: 2, z: 4, core: 2. Of those that a mesh axis runs over, the one named last changes fastest.
Arguments:
- activations: bfloat16 [4, 64, 256, 128], P('tm', 'height'), may hold values from -60 to 60
- norm_gain: float32 [128], replicated, may hold values from 0.1 to 1.9
- norm_bias: float32 [128], replicated, may hold values from -3 to 3
- conv_weight: bfloat16 [3456, 256], replicated, may hold values from -0.109375 to 0.109375
- cotangent: bfloat16 [2, 64, 256, 256], P('tm', 'height'), may hold values from -6 to 6
Outputs:
- pooled: bfloat16 [2, 64, 256, 256], P('tm', None, 'height')
- weight_grad: bfloat16 [256, 3456], P('height')
All inputs are finite; a program needn't handle non-finite values.
Results may differ from a plain program's by a relative error of at most 0.0056.
Values may be sent and summed in bfloat16 or wider, within the bound.
A program may use at most 128 MiB of HBM per device.

v0:
```python
import math
import jax
import jax.numpy as jnp
from jax import lax
from jax.sharding import PartitionSpec as P

GROUPS = 32
KT = 3


def shifted(value, axis, steps):
    count = lax.axis_size(axis)
    first, last = (max(0, -steps), min(count, count - steps))
    return lax.ppermute(value, axis, [(source, source + steps) for source in range(first, last)])


def extended(cells, sides, width):
    for axis, dim in sides:
        count = lax.axis_size(axis)
        ends = count - 1
        head = lax.slice_in_dim(cells, 0, width, axis=dim)
        tail = lax.slice_in_dim(cells, cells.shape[dim] - width, cells.shape[dim], axis=dim)
        cells = jnp.concatenate(
            [
                lax.ppermute(tail, axis, [(i, (i + 1) % count) for i in range(ends)]),
                cells,
                lax.ppermute(head, axis, [((i + 1) % count, i) for i in range(ends)]),
            ],
            axis=dim,
        )
    return cells


def pool_pairs(values):
    paired = values.reshape((values.shape[0] // 2, 2) + values.shape[1:])
    return ((paired[:, 0].astype(jnp.float32) + paired[:, 1].astype(jnp.float32)) * 0.5).astype(
        jnp.bfloat16
    )


def local(activations, norm_gain, norm_bias, conv_weight, cotangent):
    frames, rows, width, channels = activations.shape
    n_out = conv_weight.shape[1]
    per_group = channels // GROUPS
    n_time = lax.axis_size("tm")
    n_rows = lax.axis_size("height")
    entries = frames * rows * width * per_group * n_time * n_rows
    grouped = activations.reshape(frames * rows * width, GROUPS, per_group)
    local_sums = jnp.sum(grouped, axis=(0, 2), dtype=jnp.float32)
    group_mean = lax.psum(local_sums, ("tm", "height")) / entries
    centered = grouped.astype(jnp.float32) - group_mean[None, :, None]
    group_var = lax.psum(jnp.sum(centered * centered, axis=(0, 2)), ("tm", "height")) / entries
    mean_chan = jnp.repeat(group_mean, per_group)
    inv_chan = jnp.repeat(lax.rsqrt(group_var + 1e-06), per_group)
    normed = jax.nn.silu(
        (activations.astype(jnp.float32) - mean_chan) * inv_chan * norm_gain + norm_bias
    ).astype(jnp.bfloat16)
    earlier = shifted(normed, "tm", 1)
    first_frame = jnp.broadcast_to(normed[:1], earlier.shape)
    earlier = jnp.where(lax.axis_index("tm") == 0, first_frame, earlier)
    stacked = jnp.concatenate([earlier, normed], axis=0)
    padded = extended(stacked, (("height", 1),), 1)
    padded = jnp.pad(padded, ((0, 0), (0, 0), (1, 1), (0, 0)))
    patches = jnp.concatenate([padded[:, :, tap_c : tap_c + width] for tap_c in range(KT)], axis=3)
    band = KT * channels
    output = jnp.zeros((frames, rows, n_out, width), jnp.float32)
    for tap_t in range(KT):
        for tap_r in range(KT):
            start_row = (tap_t * KT + tap_r) * band
            output = output + jnp.einsum(
                "frwk,kc->frcw",
                patches[tap_t : tap_t + frames, tap_r : tap_r + rows],
                conv_weight[start_row : start_row + band],
                preferred_element_type=jnp.float32,
            )
    conv_out = output.astype(jnp.bfloat16)
    moved = lax.all_to_all(conv_out, "height", split_axis=2, concat_axis=1, tiled=True)
    pooled = pool_pairs(moved)
    upsampled = jnp.repeat(cotangent * jnp.asarray(0.5, jnp.bfloat16), 2, axis=0)
    own_rows = n_out // n_rows
    blocks = []
    for tap_t in range(KT):
        for tap_r in range(KT):
            blocks.append(
                jnp.einsum(
                    "frwk,frwc->ck",
                    patches[tap_t : tap_t + frames, tap_r : tap_r + rows],
                    upsampled,
                    preferred_element_type=jnp.float32,
                )
            )
    summed = lax.psum(jnp.concatenate(blocks, axis=1), ("tm", "height"))
    own_grad = lax.dynamic_slice_in_dim(summed, lax.axis_index("height") * own_rows, own_rows, 0)
    factor = 1.0 / math.sqrt(frames * n_time * rows * n_rows * width)
    weight_grad = (own_grad * factor).astype(jnp.bfloat16)
    return (pooled, weight_grad)


def solution(mesh):
    in_specs = (P("tm", "height", None, None), P(), P(), P(), P("tm", "height", None, None))
    out_specs = (P("tm", None, "height", None), P("height", None))
    return jax.shard_map(local, mesh=mesh, in_specs=in_specs, out_specs=out_specs, check_vma=False)
```

profile of v0, /device:TPU:0, one launch (start us, length us, event | category | flops | bytes accessed | tf_op | source)
XLA Modules:
  0.0 317.6 jit_solution(3643180153994988676)
XLA Ops:
  7.2 0.0 copy-start.2
  7.2 0.0 all-reduce.3.cloned.1.call-start
  7.2 1.4 convert_reduce_fusion
  8.6 0.1 reduce_sum.24
  8.7 0.1 reduce_sum.25
  8.8 42.0 %psum.21 = f32[32]{0:T(128)S(1)} all-reduce(f32[32]{0:T(128)S(1)} %reduce_sum.25), channel_id=1, replica_groups=mesh['tm'=2,'height'=16] {'tm','height'}, use_global_device_ids=true, to_apply=%region_2.0 | all-reduce | flops 32 | bytes 256 | tf_op jit(solution)/shard_map/psum | solution.py:50
  50.9 0.1 broadcast_in_dim.8
  50.9 0.1 sub.7
  51.0 1.3 fusion.79
  52.4 0.1 reduce_sum.36
  52.5 0.1 reduce_sum.37
  52.6 40.2 %psum.22 = f32[32]{0:T(128)S(1)} all-reduce(f32[32]{0:T(128)S(1)} %reduce_sum.37), channel_id=1, replica_groups=mesh['tm'=2,'height'=16] {'tm','height'}, use_global_device_ids=true, to_apply=%region_5.6 | all-reduce | flops 32 | bytes 256 | tf_op jit(solution)/shard_map/psum | solution.py:52
  92.8 0.1 broadcast_in_dim.18
  92.8 0.1 mul.59
  92.9 1.4 fusion.87
  94.4 4.2 %collective-permute-start = (bf16[2,4,256,128]{3,2,1,0:T(8,128)(2,1)S(1)}, bf16[2,4,256,128]{3,2,1,0:T(8,128)(2,1)S(1)}, u32[]{:S(2)}, u32[]{:S(2)}) collective-permute-start(bf16[2,4,256,128]{3,2,1,0:T(8,128)(2,1)S(1)} %fusion.87), channel_id=1, source_target_pairs={{0,16},{1,17},{2,18},{3,19},{4,20},{5,21},{6,22},{7,23},{8,24},{9,... | collective-permute-start | bytes 1572872 | tf_op jit(solution)/shard_map/ppermute | solution.py:14
  98.6 10.2 %collective-permute-done = bf16[2,4,256,128]{3,2,1,0:T(8,128)(2,1)S(1)} collective-permute-done((bf16[2,4,256,128]{3,2,1,0:T(8,128)(2,1)S(1)}, bf16[2,4,256,128]{3,2,1,0:T(8,128)(2,1)S(1)}, u32[]{:S(2)}, u32[]{:S(2)}) %collective-permute-start) | collective-permute-done | bytes 524320 | tf_op jit(solution)/shard_map/ppermute | solution.py:14
  109.0 1.3 collective-permute-start.2
  110.3 3.0 collective-permute-start.1
  113.3 0.0 copy-done.2
  113.4 0.2 copy.17
  113.6 0.0 collective-permute-done.2
  113.6 0.8 collective-permute-done.1
  114.5 0.5 select_maximum_fusion
  114.9 1.1 fusion.124
  116.0 0.0 copy-start.1
  116.0 2.1 pad_maximum_fusion
  118.1 0.0 copy-done.1
  118.1 0.0 copy-start
  118.1 0.7 fusion.99
  118.8 2.2 fusion.101
  121.0 2.0 fusion.103
  123.0 2.0 fusion.105
  125.0 2.0 fusion.107
  127.0 2.1 fusion.109
  129.1 2.1 fusion.113
  131.1 2.1 fusion.111
  133.2 1.5 fusion.28
  134.7 1.5 fusion.34
  136.2 1.5 fusion.40
  137.8 1.5 fusion.46
  139.3 1.5 fusion.52
  140.7 1.5 fusion.58
  142.3 1.6 fusion.64
  143.8 1.5 fusion.70
  145.3 0.0 copy-done
  145.3 1.5 fusion.76
  146.8 0.0 all-reduce.3.cloned.1.call-update
  146.9 6.7 %fusion.22 = bf16[2,4,256,256]{2,3,1,0:T(8,128)(2,1)S(1)} fusion(bf16[4,6,256,384]{3,2,1,0:T(8,128)(2,1)} %copy-done, f32[2,4,256,256]{3,2,1,0:T(8,128)S(1)} %fusion.99, f32[2,4,256,256]{3,2,1,0:T(8,128)} %fusion.101, f32[2,4,256,256]{3,2,1,0:T(8,128)} %fusion.103, f32[2,4,256,256]{3,2,1,0:T(8,128)} %fusion.105, f32[2,4,256,256]{3,2,1,0:T(8,128)} %fusion.107, ...), kind=kOutput, calls=%fused_computation.28 | convolution fusion | flops 407371776 | bytes 22740992 | tf_op jit(solution)/shard_map/frwk,kc->frcw/dot_general | solution.py:70
  153.6 1.8 copy.14
  155.4 8.7 %all-to-all-start = ((bf16[2,4,256,256]{3,1,0,2:T(4,128)(2,1)}), bf16[2,4,256,256]{3,1,0,2:T(4,128)(2,1)S(1)}, u32[]{:S(2)}, u32[]{:S(2)}) async-start(bf16[2,4,256,256]{3,1,0,2:T(4,128)(2,1)} %copy.14), calls=%async_computation | async-start | bytes 2097152 | tf_op jit(solution)/shard_map/all_to_all | solution.py:77
  164.2 143.7 %all-reduce.3.cloned.1.call-done = f32[256,3456]{1,0:T(8,128)} async-done(((f32[256,3456]{1,0:T(8,128)}), f32[256,3456]{1,0:T(8,128)}) %all-reduce.3.cloned.1.call-update) | async-done | bytes 3538960 | tf_op jit(solution)/shard_map/psum | solution.py:92
  307.8 1.6 multiply_convert_fusion.1
  309.4 0.0 all-to-all-done
  309.4 0.2 copy.15
  309.6 0.1 copy.16
  309.8 1.0 fusion.88
  (6 shorter events, 0.2 us)
Async XLA Ops:
  7.2 106.2 %copy-start.2 = (bf16[1,4,256,256]{3,2,1,0:T(8,128)(2,1)S(1)}, bf16[1,4,256,256]{3,2,1,0:T(8,128)(2,1)}, u32[]{:S(2)}) copy-start(bf16[1,4,256,256]{3,2,1,0:T(8,128)(2,1)} %param.9) | copy-start | bytes 1572868
  7.2 300.7 %all-reduce.3.cloned.1.call-start = ((), (), s32[]{:S(2)}) async-start(), calls=%async_computation.1 | async-start | bytes 7077888 | tf_op jit(solution)/shard_map/psum | solution.py:92
  94.4 14.5 %collective-permute-start = (bf16[2,4,256,128]{3,2,1,0:T(8,128)(2,1)S(1)}, bf16[2,4,256,128]{3,2,1,0:T(8,128)(2,1)S(1)}, u32[]{:S(2)}, u32[]{:S(2)}) collective-permute-start(bf16[2,4,256,128]{3,2,1,0:T(8,128)(2,1)S(1)} %fusion.87), channel_id=1, source_target_pairs={{0,16},{1,17},{2,18},{3,19},{4,20},{5,21},{6,22},{7,23},{8,24},{9,... | collective-permute-start | bytes 1572872 | tf_op jit(solution)/shard_map/ppermute | solution.py:14
  109.0 4.6 %collective-permute-start.2 = (bf16[4,1,256,128]{3,2,1,0:T(8,128)(2,1)S(1)}, bf16[4,1,256,128]{3,2,1,0:T(8,128)(2,1)S(1)}, u32[]{:S(2)}, u32[]{:S(2)}) collective-permute-start(bf16[4,1,256,128]{3,2,1,0:T(8,128)(2,1)S(1)} %get-tuple-element.5), channel_id=1, source_target_pairs={{1,0},{2,1},{3,2},{4,3},{5,4},{6,5},{7,6},{8,7},{9,8},{10,9},{11,1... | collective-permute-start | bytes 786440 | tf_op jit(solution)/shard_map/ppermute | solution.py:27
  110.3 4.2 %collective-permute-start.1 = (bf16[4,1,256,128]{3,2,1,0:T(8,128)(2,1)S(1)}, bf16[4,1,256,128]{3,2,1,0:T(8,128)(2,1)S(1)}, u32[]{:S(2)}, u32[]{:S(2)}) collective-permute-start(bf16[4,1,256,128]{3,2,1,0:T(8,128)(2,1)S(1)} %get-tuple-element.4), channel_id=1, source_target_pairs={{0,1},{1,2},{2,3},{3,4},{4,5},{5,6},{6,7},{7,8},{8,9},{9,10},{10,1... | collective-permute-start | bytes 786440 | tf_op jit(solution)/shard_map/ppermute | solution.py:25
  116.0 2.1 copy-start.1
  118.1 27.2 %copy-start = (bf16[4,6,256,384]{3,2,1,0:T(8,128)(2,1)}, bf16[4,6,256,384]{3,2,1,0:T(8,128)(2,1)S(1)}, u32[]{:S(2)}) copy-start(bf16[4,6,256,384]{3,2,1,0:T(8,128)(2,1)S(1)} %pad_maximum_fusion) | copy-start | bytes 14155780
  155.4 154.0 %all-to-all-start = ((bf16[2,4,256,256]{3,1,0,2:T(4,128)(2,1)}), bf16[2,4,256,256]{3,1,0,2:T(4,128)(2,1)S(1)}, u32[]{:S(2)}, u32[]{:S(2)}) async-start(bf16[2,4,256,256]{3,1,0,2:T(4,128)(2,1)} %copy.14), calls=%async_computation | async-start | bytes 2097152 | tf_op jit(solution)/shard_map/all_to_all | solution.py:77
Sparse Core Ops, SparseCore 0:
  147.0 160.7 all-reduce.2
where the time goes:
time: 318 us
  waiting for transfers between devices  155 us (49%)
  blocking collectives  82.2 us (26%)
  matrix products  35.4 us (11%)
  starting transfers between devices  17.3 us (5%)
  between operations  14.2 us (4%)
  other arithmetic  9.63 us (3%)
  local copies, waits for them, and re-layouts  4.02 us (1%)
    psum x1, waiting for transfers between devices, local(): summed = lax.psum(jnp.concatenate(blocks, axis=1), ('tm', 'height'))  144 us
    psum x1, blocking collectives, local(): group_mean = lax.psum(local_sums, ('tm', 'height')) / entries  42 us
    psum x1, blocking collectives, local(): lax.psum(jnp.sum(centered * centered, axis=(0, 2)), ('tm', 'height'))  40.2 us
    dot_general x9, matrix products, local(): jnp.einsum('frwk,kc->frcw', patches[tap_t:tap_t + frames, tap_r:tap_r + r...  21.8 us
    dot_general x9, matrix products, local(): jnp.einsum('frwk,frwc->ck', patches[tap_t:tap_t + frames, tap_r:tap_r + r...  13.6 us
    ppermute x1, waiting for transfers between devices, shifted(): lax.ppermute(value, axis, [(source, source + steps) for source in range(f...  10.2 us
    all_to_all x1, starting transfers between devices, local(): lax.all_to_all(conv_out, 'height', split_axis=2, concat_axis=1, tiled=True)  8.75 us
  transfers between devices with their start and end apart: 5, of which 3 were waited for; matrix products, arithmetic and copies ran while one was open for 3% of the time, Pallas kernels for 0%

commit v1 on v0

--- a/solution.py
+++ b/solution.py
@@ -6,6 +6,17 @@
 
 GROUPS = 32
 KT = 3
+
+
+def in_blocks(x, dim, count):
+    before, after = (x.shape[:dim], x.shape[dim + 1 :])
+    return jnp.moveaxis(x.reshape(*before, count, -1, *after), dim, 0)
+
+
+def joined_along(blocks, dim):
+    blocks = jnp.moveaxis(blocks, 0, dim)
+    shape = blocks.shape
+    return blocks.reshape(*shape[:dim], shape[dim] * shape[dim + 1], *shape[dim + 2 :])
 
 
 def shifted(value, axis, steps):
@@ -74,7 +85,15 @@
                 preferred_element_type=jnp.float32,
             )
     conv_out = output.astype(jnp.bfloat16)
-    moved = lax.all_to_all(conv_out, "height", split_axis=2, concat_axis=1, tiled=True)
+    peers, position = (lax.axis_size("height"), lax.axis_index("height"))
+    pieces = in_blocks(conv_out, 2, peers)
+    out = pieces
+    for step in range(1, peers):
+        target, source_2 = ((position + step) % peers, (position - step) % peers)
+        sent = lax.dynamic_index_in_dim(pieces, target, 0)
+        other = lax.ppermute(sent, "height", [(i_2, (i_2 + step) % peers) for i_2 in range(peers)])
+        out = lax.dynamic_update_slice_in_dim(out, other, source_2, axis=0)
+    moved = joined_along(out, 1)
     pooled = pool_pairs(moved)
     upsampled = jnp.repeat(cotangent * jnp.asarray(0.5, jnp.bfloat16), 2, axis=0)
     own_rows = n_out // n_rows

time: 318 us -> 309 us (0.972)
  starting transfers between devices: 17.3 us -> 39.7 us
  waiting for transfers between devices: 155 us -> 138 us
  matrix products: 35.4 us -> 20.9 us
    ppermute x0 -> x15, starting transfers between devices: none -> 31 us  [local(): lax.ppermute(sent, 'height', [(i_2, (i_2 + step) % peers) for i_2 in rang...]
    psum x1, waiting for transfers between devices: 144 us -> 121 us  [local(): summed = lax.psum(jnp.concatenate(blocks, axis=1), ('tm', 'height'))]
    dot_general x9, matrix products: 21.8 us -> 7.32 us  [local(): jnp.einsum('frwk,kc->frcw', patches[tap_t:tap_t + frames, tap_r:tap_r + r...]
    all_to_all x1 -> x0, starting transfers between devices: 8.75 us -> none  [local(): lax.all_to_all(conv_out, 'height', split_axis=2, concat_axis=1, tiled=True)]
    ppermute x0 -> x15, waiting for transfers between devices: none -> 7.09 us  [local(): lax.ppermute(sent, 'height', [(i_2, (i_2 + step) % peers) for i_2 in rang...]
  transfers between devices with their start and end apart: 5 -> 19, of which waited for: 3 -> 6; matrix products, arithmetic and copies ran while one was open for 3% -> 5% of each run, Pallas kernels for 0% -> 0%
where the time goes in v1:
time: 309 us; the launch traced here: 308 us
  waiting for transfers between devices  138 us (45%)
  blocking collectives  82.2 us (27%)
  starting transfers between devices  39.7 us (13%)
  matrix products  20.9 us (7%)
  between operations  15 us (5%)
  other arithmetic  9.45 us (3%)
    psum x1, waiting for transfers between devices, local(): summed = lax.psum(jnp.concatenate(blocks, axis=1), ('tm', 'height'))  121 us
    psum x1, blocking collectives, local(): group_mean = lax.psum(local_sums, ('tm', 'height')) / entries  42 us
    psum x1, blocking collectives, local(): lax.psum(jnp.sum(centered * centered, axis=(0, 2)), ('tm', 'height'))  40.2 us
    ppermute x15, starting transfers between devices, local(): lax.ppermute(sent, 'height', [(i_2, (i_2 + step) % peers) for i_2 in rang...  31 us
    dot_general x9, matrix products, local(): jnp.einsum('frwk,frwc->ck', patches[tap_t:tap_t + frames, tap_r:tap_r + r...  13.6 us
    ppermute x1, waiting for transfers between devices, shifted(): lax.ppermute(value, axis, [(source, source + steps) for source in range(f...  10 us
    dot_general x9, matrix products, local(): jnp.einsum('frwk,kc->frcw', patches[tap_t:tap_t + frames, tap_r:tap_r + r...  7.32 us
    ppermute x15, waiting for transfers between devices, local(): lax.ppermute(sent, 'height', [(i_2, (i_2 + step) % peers) for i_2 in rang...  7.09 us
  transfers between devices with their start and end apart: 19, of which 6 were waited for; matrix products, arithmetic and copies ran while one was open for 5% of the time, Pallas kernels for 0%

profile of v1, /device:TPU:0, one launch (start us, length us, event | category | flops | bytes accessed | tf_op | source)
XLA Modules:
  0.0 308.0 jit_solution(13479069004258072851)
XLA Ops:
  7.2 0.0 all-reduce.3.cloned.1.call-start
  7.2 1.4 convert_reduce_fusion
  8.6 0.1 reduce_sum.24
  8.7 0.1 reduce_sum.25
  8.8 42.0 %psum.21 = f32[32]{0:T(128)S(1)} all-reduce(f32[32]{0:T(128)S(1)} %reduce_sum.25), channel_id=1, replica_groups=mesh['tm'=2,'height'=16] {'tm','height'}, use_global_device_ids=true, to_apply=%region_2.0 | all-reduce | flops 32 | bytes 256 | tf_op jit(solution)/shard_map/psum | solution.py:61
  50.8 0.1 broadcast_in_dim.8
  50.9 0.1 sub.60
  51.0 1.3 fusion.78
  52.4 0.1 reduce_sum.36
  52.5 0.1 reduce_sum.37
  52.6 40.2 %psum.22 = f32[32]{0:T(128)S(1)} all-reduce(f32[32]{0:T(128)S(1)} %reduce_sum.37), channel_id=1, replica_groups=mesh['tm'=2,'height'=16] {'tm','height'}, use_global_device_ids=true, to_apply=%region_5.6 | all-reduce | flops 32 | bytes 256 | tf_op jit(solution)/shard_map/psum | solution.py:63
  92.7 0.1 broadcast_in_dim.18
  92.8 0.1 mul.59
  92.9 1.4 fusion.86
  94.4 4.2 %collective-permute-start = (bf16[2,4,256,128]{3,2,1,0:T(8,128)(2,1)S(1)}, bf16[2,4,256,128]{3,2,1,0:T(8,128)(2,1)S(1)}, u32[]{:S(2)}, u32[]{:S(2)}) collective-permute-start(bf16[2,4,256,128]{3,2,1,0:T(8,128)(2,1)S(1)} %fusion.86), channel_id=1, source_target_pairs={{0,16},{1,17},{2,18},{3,19},{4,20},{5,21},{6,22},{7,23},{8,24},{9,... | collective-permute-start | bytes 1572872 | tf_op jit(solution)/shard_map/ppermute | solution.py:25
  98.8 10.0 %collective-permute-done = bf16[2,4,256,128]{3,2,1,0:T(8,128)(2,1)S(1)} collective-permute-done((bf16[2,4,256,128]{3,2,1,0:T(8,128)(2,1)S(1)}, bf16[2,4,256,128]{3,2,1,0:T(8,128)(2,1)S(1)}, u32[]{:S(2)}, u32[]{:S(2)}) %collective-permute-start) | collective-permute-done | bytes 524320 | tf_op jit(solution)/shard_map/ppermute | solution.py:25
  109.0 1.3 collective-permute-start.2
  110.3 3.2 %collective-permute-start.1 = (bf16[4,1,256,128]{3,2,1,0:T(8,128)(2,1)S(1)}, bf16[4,1,256,128]{3,2,1,0:T(8,128)(2,1)S(1)}, u32[]{:S(2)}, u32[]{:S(2)}) collective-permute-start(bf16[4,1,256,128]{3,2,1,0:T(8,128)(2,1)S(1)} %get-tuple-element.19), channel_id=1, source_target_pairs={{0,1},{1,2},{2,3},{3,4},{4,5},{5,6},{6,7},{7,8},{8,9},{9,10},{10,1... | collective-permute-start | bytes 786440 | tf_op jit(solution)/shard_map/ppermute | solution.py:36
  113.8 0.2 copy.28
  114.2 0.2 collective-permute-done.1
  114.4 0.5 select_maximum_fusion
  114.9 1.1 fusion.123
  116.0 0.0 copy-start
  116.0 1.9 pad_maximum_fusion
  117.9 0.8 fusion.98
  118.7 0.8 fusion.100
  119.4 0.8 fusion.102
  120.2 0.8 fusion.104
  121.0 0.8 fusion.106
  121.7 0.8 fusion.108
  122.5 0.8 fusion.112
  123.2 0.8 fusion.110
  124.0 1.3 add_convert_fusion
  125.3 0.2 dynamic-slice_bitcast_fusion
  125.4 3.3 %collective-permute-start.3 = (bf16[1,2,4,16,256]{4,3,0,2,1:T(8,128)(2,1)S(1)}, bf16[1,2,4,16,256]{4,3,0,2,1:T(8,128)(2,1)S(1)}, u32[]{:S(2)}, u32[]{:S(2)}) collective-permute-start(bf16[1,2,4,16,256]{4,3,0,2,1:T(8,128)(2,1)S(1)} %get-tuple-element.18), channel_id=1, source_target_pairs={{0,1},{1,2},{2,3},{3,4},{4,5},{5,6},{6,7},{7,8},{8,9},{9,10},{10,1... | collective-permute-start | bytes 196616 | tf_op jit(solution)/shard_map/ppermute | solution.py:94
  128.7 2.4 collective-permute-start.4
  131.1 2.1 collective-permute-start.5
  133.2 1.7 collective-permute-start.6
  134.9 1.5 fusion.27
  136.4 1.5 fusion.33
  137.9 1.5 fusion.39
  139.5 1.5 fusion.45
  140.9 1.5 fusion.51
  142.5 1.5 fusion.57
  144.0 1.5 fusion.63
  145.5 1.5 fusion.69
  147.0 1.5 fusion.75
  148.5 0.0 all-reduce.3.cloned.1.call-update
  148.5 1.6 collective-permute-start.8
  150.1 4.1 %collective-permute-start.9 = (bf16[1,2,4,16,256]{4,3,0,2,1:T(8,128)(2,1)S(1)}, bf16[1,2,4,16,256]{4,3,0,2,1:T(8,128)(2,1)S(1)}, u32[]{:S(2)}, u32[]{:S(2)}) collective-permute-start(bf16[1,2,4,16,256]{4,3,0,2,1:T(8,128)(2,1)S(1)} %get-tuple-element.12), channel_id=1, source_target_pairs={{0,7},{1,8},{2,9},{3,10},{4,11},{5,12},{6,13},{7,14},{8,15},{9,0},... | collective-permute-start | bytes 196616 | tf_op jit(solution)/shard_map/ppermute | solution.py:94
  154.3 0.6 collective-permute-start.10
  155.0 0.1 collective-permute-start.11
  155.1 1.5 collective-permute-start.12
  156.6 2.4 collective-permute-done.8
  159.0 1.8 collective-permute-start.13
  160.8 2.5 collective-permute-start.14
  163.3 2.0 collective-permute-done.10
  165.3 5.5 %collective-permute-start.16 = (bf16[1,2,4,16,256]{4,3,0,2,1:T(8,128)(2,1)S(1)}, bf16[1,2,4,16,256]{4,3,0,2,1:T(8,128)(2,1)S(1)}, u32[]{:S(2)}, u32[]{:S(2)}) collective-permute-start(bf16[1,2,4,16,256]{4,3,0,2,1:T(8,128)(2,1)S(1)} %get-tuple-element.5), channel_id=1, source_target_pairs={{0,14},{1,15},{2,0},{3,1},{4,2},{5,3},{6,4},{7,5},{8,6},{9,7},{10,... | collective-permute-start | bytes 196616 | tf_op jit(solution)/shard_map/ppermute | solution.py:94
  170.8 3.9 %collective-permute-start.17 = (bf16[1,2,4,16,256]{4,3,0,2,1:T(8,128)(2,1)S(1)}, bf16[1,2,4,16,256]{4,3,0,2,1:T(8,128)(2,1)S(1)}, u32[]{:S(2)}, u32[]{:S(2)}) collective-permute-start(bf16[1,2,4,16,256]{4,3,0,2,1:T(8,128)(2,1)S(1)} %get-tuple-element.4), channel_id=1, source_target_pairs={{0,15},{1,0},{2,1},{3,2},{4,3},{5,4},{6,5},{7,6},{8,7},{9,8},{10,9... | collective-permute-start | bytes 196616 | tf_op jit(solution)/shard_map/ppermute | solution.py:94
  174.7 2.7 collective-permute-done.16
  177.4 0.1 copy.27
  177.6 1.0 fusion.87
  178.5 121.0 %all-reduce.3.cloned.1.call-done = f32[256,3456]{1,0:T(8,128)} async-done(((f32[256,3456]{1,0:T(8,128)}), f32[256,3456]{1,0:T(8,128)}) %all-reduce.3.cloned.1.call-update) | async-done | bytes 3538960 | tf_op jit(solution)/shard_map/psum | solution.py:111
  299.6 1.6 multiply_convert_fusion.1
  (39 shorter events, 0.4 us)
Async XLA Ops:
  7.2 106.6 %copy-start.1 = (bf16[1,4,256,256]{3,2,1,0:T(8,128)(2,1)S(1)}, bf16[1,4,256,256]{3,2,1,0:T(8,128)(2,1)}, u32[]{:S(2)}) copy-start(bf16[1,4,256,256]{3,2,1,0:T(8,128)(2,1)} %param.9) | copy-start | bytes 1572868
  7.2 292.4 %all-reduce.3.cloned.1.call-start = ((), (), s32[]{:S(2)}) async-start(), calls=%async_computation | async-start | bytes 7077888 | tf_op jit(solution)/shard_map/psum | solution.py:111
  94.4 14.5 %collective-permute-start = (bf16[2,4,256,128]{3,2,1,0:T(8,128)(2,1)S(1)}, bf16[2,4,256,128]{3,2,1,0:T(8,128)(2,1)S(1)}, u32[]{:S(2)}, u32[]{:S(2)}) collective-permute-start(bf16[2,4,256,128]{3,2,1,0:T(8,128)(2,1)S(1)} %fusion.86), channel_id=1, source_target_pairs={{0,16},{1,17},{2,18},{3,19},{4,20},{5,21},{6,22},{7,23},{8,24},{9,... | collective-permute-start | bytes 1572872 | tf_op jit(solution)/shard_map/ppermute | solution.py:25
  109.0 5.2 %collective-permute-start.2 = (bf16[4,1,256,128]{3,2,1,0:T(8,128)(2,1)S(1)}, bf16[4,1,256,128]{3,2,1,0:T(8,128)(2,1)S(1)}, u32[]{:S(2)}, u32[]{:S(2)}) collective-permute-start(bf16[4,1,256,128]{3,2,1,0:T(8,128)(2,1)S(1)} %get-tuple-element.20), channel_id=1, source_target_pairs={{1,0},{2,1},{3,2},{4,3},{5,4},{6,5},{7,6},{8,7},{9,8},{10,9},{11,1... | collective-permute-start | bytes 786440 | tf_op jit(solution)/shard_map/ppermute | solution.py:38
  110.3 4.2 %collective-permute-start.1 = (bf16[4,1,256,128]{3,2,1,0:T(8,128)(2,1)S(1)}, bf16[4,1,256,128]{3,2,1,0:T(8,128)(2,1)S(1)}, u32[]{:S(2)}, u32[]{:S(2)}) collective-permute-start(bf16[4,1,256,128]{3,2,1,0:T(8,128)(2,1)S(1)} %get-tuple-element.19), channel_id=1, source_target_pairs={{0,1},{1,2},{2,3},{3,4},{4,5},{5,6},{6,7},{7,8},{8,9},{9,10},{10,1... | collective-permute-start | bytes 786440 | tf_op jit(solution)/shard_map/ppermute | solution.py:36
  116.0 1.9 copy-start
  125.4 23.1 %collective-permute-start.3 = (bf16[1,2,4,16,256]{4,3,0,2,1:T(8,128)(2,1)S(1)}, bf16[1,2,4,16,256]{4,3,0,2,1:T(8,128)(2,1)S(1)}, u32[]{:S(2)}, u32[]{:S(2)}) collective-permute-start(bf16[1,2,4,16,256]{4,3,0,2,1:T(8,128)(2,1)S(1)} %get-tuple-element.18), channel_id=1, source_target_pairs={{0,1},{1,2},{2,3},{3,4},{4,5},{5,6},{6,7},{7,8},{8,9},{9,10},{10,1... | collective-permute-start | bytes 196616 | tf_op jit(solution)/shard_map/ppermute | solution.py:94
  128.7 21.4 %collective-permute-start.4 = (bf16[1,2,4,16,256]{4,3,0,2,1:T(8,128)(2,1)S(1)}, bf16[1,2,4,16,256]{4,3,0,2,1:T(8,128)(2,1)S(1)}, u32[]{:S(2)}, u32[]{:S(2)}) collective-permute-start(bf16[1,2,4,16,256]{4,3,0,2,1:T(8,128)(2,1)S(1)} %get-tuple-element.17), channel_id=1, source_target_pairs={{0,2},{1,3},{2,4},{3,5},{4,6},{5,7},{6,8},{7,9},{8,10},{9,11},{10,... | collective-permute-start | bytes 196616 | tf_op jit(solution)/shard_map/ppermute | solution.py:94
  131.1 23.2 %collective-permute-start.5 = (bf16[1,2,4,16,256]{4,3,0,2,1:T(8,128)(2,1)S(1)}, bf16[1,2,4,16,256]{4,3,0,2,1:T(8,128)(2,1)S(1)}, u32[]{:S(2)}, u32[]{:S(2)}) collective-permute-start(bf16[1,2,4,16,256]{4,3,0,2,1:T(8,128)(2,1)S(1)} %get-tuple-element.16), channel_id=1, source_target_pairs={{0,3},{1,4},{2,5},{3,6},{4,7},{5,8},{6,9},{7,10},{8,11},{9,12},{10... | collective-permute-start | bytes 196616 | tf_op jit(solution)/shard_map/ppermute | solution.py:94
  133.2 21.7 %collective-permute-start.6 = (bf16[1,2,4,16,256]{4,3,0,2,1:T(8,128)(2,1)S(1)}, bf16[1,2,4,16,256]{4,3,0,2,1:T(8,128)(2,1)S(1)}, u32[]{:S(2)}, u32[]{:S(2)}) collective-permute-start(bf16[1,2,4,16,256]{4,3,0,2,1:T(8,128)(2,1)S(1)} %get-tuple-element.15), channel_id=1, source_target_pairs={{0,4},{1,5},{2,6},{3,7},{4,8},{5,9},{6,10},{7,11},{8,12},{9,13},{1... | collective-permute-start | bytes 196616 | tf_op jit(solution)/shard_map/ppermute | solution.py:94
  134.9 20.2 %collective-permute-start.7 = (bf16[1,2,4,16,256]{4,3,0,2,1:T(8,128)(2,1)S(1)}, bf16[1,2,4,16,256]{4,3,0,2,1:T(8,128)(2,1)S(1)}, u32[]{:S(2)}, u32[]{:S(2)}) collective-permute-start(bf16[1,2,4,16,256]{4,3,0,2,1:T(8,128)(2,1)S(1)} %get-tuple-element.14), channel_id=1, source_target_pairs={{0,5},{1,6},{2,7},{3,8},{4,9},{5,10},{6,11},{7,12},{8,13},{9,14},{... | collective-permute-start | bytes 196616 | tf_op jit(solution)/shard_map/ppermute | solution.py:94
  148.5 10.4 %collective-permute-start.8 = (bf16[1,2,4,16,256]{4,3,0,2,1:T(8,128)(2,1)S(1)}, bf16[1,2,4,16,256]{4,3,0,2,1:T(8,128)(2,1)S(1)}, u32[]{:S(2)}, u32[]{:S(2)}) collective-permute-start(bf16[1,2,4,16,256]{4,3,0,2,1:T(8,128)(2,1)S(1)} %get-tuple-element.13), channel_id=1, source_target_pairs={{0,6},{1,7},{2,8},{3,9},{4,10},{5,11},{6,12},{7,13},{8,14},{9,15},... | collective-permute-start | bytes 196616 | tf_op jit(solution)/shard_map/ppermute | solution.py:94
  150.1 10.6 %collective-permute-start.9 = (bf16[1,2,4,16,256]{4,3,0,2,1:T(8,128)(2,1)S(1)}, bf16[1,2,4,16,256]{4,3,0,2,1:T(8,128)(2,1)S(1)}, u32[]{:S(2)}, u32[]{:S(2)}) collective-permute-start(bf16[1,2,4,16,256]{4,3,0,2,1:T(8,128)(2,1)S(1)} %get-tuple-element.12), channel_id=1, source_target_pairs={{0,7},{1,8},{2,9},{3,10},{4,11},{5,12},{6,13},{7,14},{8,15},{9,0},... | collective-permute-start | bytes 196616 | tf_op jit(solution)/shard_map/ppermute | solution.py:94
  154.3 10.9 %collective-permute-start.10 = (bf16[1,2,4,16,256]{4,3,0,2,1:T(8,128)(2,1)S(1)}, bf16[1,2,4,16,256]{4,3,0,2,1:T(8,128)(2,1)S(1)}, u32[]{:S(2)}, u32[]{:S(2)}) collective-permute-start(bf16[1,2,4,16,256]{4,3,0,2,1:T(8,128)(2,1)S(1)} %get-tuple-element.11), channel_id=1, source_target_pairs={{0,8},{1,9},{2,10},{3,11},{4,12},{5,13},{6,14},{7,15},{8,0},{9,1},... | collective-permute-start | bytes 196616 | tf_op jit(solution)/shard_map/ppermute | solution.py:94
  155.0 10.3 %collective-permute-start.11 = (bf16[1,2,4,16,256]{4,3,0,2,1:T(8,128)(2,1)S(1)}, bf16[1,2,4,16,256]{4,3,0,2,1:T(8,128)(2,1)S(1)}, u32[]{:S(2)}, u32[]{:S(2)}) collective-permute-start(bf16[1,2,4,16,256]{4,3,0,2,1:T(8,128)(2,1)S(1)} %get-tuple-element.10), channel_id=1, source_target_pairs={{0,9},{1,10},{2,11},{3,12},{4,13},{5,14},{6,15},{7,0},{8,1},{9,2},... | collective-permute-start | bytes 196616 | tf_op jit(solution)/shard_map/ppermute | solution.py:94
  155.1 15.7 %collective-permute-start.12 = (bf16[1,2,4,16,256]{4,3,0,2,1:T(8,128)(2,1)S(1)}, bf16[1,2,4,16,256]{4,3,0,2,1:T(8,128)(2,1)S(1)}, u32[]{:S(2)}, u32[]{:S(2)}) collective-permute-start(bf16[1,2,4,16,256]{4,3,0,2,1:T(8,128)(2,1)S(1)} %get-tuple-element.9), channel_id=1, source_target_pairs={{0,10},{1,11},{2,12},{3,13},{4,14},{5,15},{6,0},{7,1},{8,2},{9,3},... | collective-permute-start | bytes 196616 | tf_op jit(solution)/shard_map/ppermute | solution.py:94
  159.0 15.7 %collective-permute-start.13 = (bf16[1,2,4,16,256]{4,3,0,2,1:T(8,128)(2,1)S(1)}, bf16[1,2,4,16,256]{4,3,0,2,1:T(8,128)(2,1)S(1)}, u32[]{:S(2)}, u32[]{:S(2)}) collective-permute-start(bf16[1,2,4,16,256]{4,3,0,2,1:T(8,128)(2,1)S(1)} %get-tuple-element.8), channel_id=1, source_target_pairs={{0,11},{1,12},{2,13},{3,14},{4,15},{5,0},{6,1},{7,2},{8,3},{9,4},{... | collective-permute-start | bytes 196616 | tf_op jit(solution)/shard_map/ppermute | solution.py:94
  160.8 13.9 %collective-permute-start.14 = (bf16[1,2,4,16,256]{4,3,0,2,1:T(8,128)(2,1)S(1)}, bf16[1,2,4,16,256]{4,3,0,2,1:T(8,128)(2,1)S(1)}, u32[]{:S(2)}, u32[]{:S(2)}) collective-permute-start(bf16[1,2,4,16,256]{4,3,0,2,1:T(8,128)(2,1)S(1)} %get-tuple-element.7), channel_id=1, source_target_pairs={{0,12},{1,13},{2,14},{3,15},{4,0},{5,1},{6,2},{7,3},{8,4},{9,5},{1... | collective-permute-start | bytes 196616 | tf_op jit(solution)/shard_map/ppermute | solution.py:94
  165.2 9.4 %collective-permute-start.15 = (bf16[1,2,4,16,256]{4,3,0,2,1:T(8,128)(2,1)S(1)}, bf16[1,2,4,16,256]{4,3,0,2,1:T(8,128)(2,1)S(1)}, u32[]{:S(2)}, u32[]{:S(2)}) collective-permute-start(bf16[1,2,4,16,256]{4,3,0,2,1:T(8,128)(2,1)S(1)} %get-tuple-element.6), channel_id=1, source_target_pairs={{0,13},{1,14},{2,15},{3,0},{4,1},{5,2},{6,3},{7,4},{8,5},{9,6},{10... | collective-permute-start | bytes 196616 | tf_op jit(solution)/shard_map/ppermute | solution.py:94
  165.3 12.1 %collective-permute-start.16 = (bf16[1,2,4,16,256]{4,3,0,2,1:T(8,128)(2,1)S(1)}, bf16[1,2,4,16,256]{4,3,0,2,1:T(8,128)(2,1)S(1)}, u32[]{:S(2)}, u32[]{:S(2)}) collective-permute-start(bf16[1,2,4,16,256]{4,3,0,2,1:T(8,128)(2,1)S(1)} %get-tuple-element.5), channel_id=1, source_target_pairs={{0,14},{1,15},{2,0},{3,1},{4,2},{5,3},{6,4},{7,5},{8,6},{9,7},{10,... | collective-permute-start | bytes 196616 | tf_op jit(solution)/shard_map/ppermute | solution.py:94
  170.8 6.6 %collective-permute-start.17 = (bf16[1,2,4,16,256]{4,3,0,2,1:T(8,128)(2,1)S(1)}, bf16[1,2,4,16,256]{4,3,0,2,1:T(8,128)(2,1)S(1)}, u32[]{:S(2)}, u32[]{:S(2)}) collective-permute-start(bf16[1,2,4,16,256]{4,3,0,2,1:T(8,128)(2,1)S(1)} %get-tuple-element.4), channel_id=1, source_target_pairs={{0,15},{1,0},{2,1},{3,2},{4,3},{5,4},{6,5},{7,6},{8,7},{9,8},{10,9... | collective-permute-start | bytes 196616 | tf_op jit(solution)/shard_map/ppermute | solution.py:94
Sparse Core Ops, SparseCore 0:
  148.7 150.8 all-reduce.2
